TPU v7x, 256 devices: a whole 4x4x8 slice. The times are simulated.
256 devices in a mesh: row: 8 (over y, core), col: 32 (over x, z).
Axes of the slice: x: 4, y: 4, z: 8, core: 2. Of those that a mesh axis runs over, the one named last changes fastest.
Arguments:
- tokens: bfloat16 [2048, 6144], P('row', 'col'), may hold values from -6 to 6
- cotangent: bfloat16 [2048, 6144], P('row', 'col'), may hold values from -6 to 6
- w_expand: bfloat16 [6144, 12288], P('row', 'col'), may hold values from -0.078125 to 0.078125
- w_reduce: bfloat16 [6144, 12288], P('row', 'col'), may hold values from -0.0546875 to 0.0546875
- expand_mean: bfloat16 [6144, 12288], P('row', 'col'), may hold values from -1 to 1
- expand_mean_scale: float32 [24, 12288], P('row', 'col'), may hold values from 4 to 16
- expand_var: bfloat16 [6144, 12288], P('row', 'col'), may hold values from 0.049804688 to 1
- expand_var_scale: float32 [24, 12288], P('row', 'col'), may hold values from 4 to 16
- reduce_mean: bfloat16 [6144, 12288], P('row', 'col'), may hold values from -1 to 1
- reduce_mean_scale: float32 [24, 12288], P('row', 'col'), may hold values from 4 to 16
- reduce_var: bfloat16 [6144, 12288], P('row', 'col'), may hold values from 0.049804688 to 1
- reduce_var_scale: float32 [24, 12288], P('row', 'col'), may hold values from 4 to 16
Outputs:
- grad_tokens: bfloat16 [2048, 6144], P('row', 'col')
- new_expand: bfloat16 [6144, 12288], P('row', 'col')
- expand_mean_next: bfloat16 [6144, 12288], P('row', 'col')
- expand_mean_scale_next: float32 [24, 12288], P('row', 'col')
- expand_var_next: bfloat16 [6144, 12288], P('row', 'col')
- expand_var_scale_next: float32 [24, 12288], P('row', 'col')
- new_reduce: bfloat16 [6144, 12288], P('row', 'col')
- reduce_mean_next: bfloat16 [6144, 12288], P('row', 'col')
- reduce_mean_scale_next: float32 [24, 12288], P('row', 'col')
- reduce_var_next: bfloat16 [6144, 12288], P('row', 'col')
- reduce_var_scale_next: float32 [24, 12288], P('row', 'col')
All inputs are finite; a program needn't handle non-finite values.
Results may differ from a plain program's by a relative error of at most 0.0049.
Values may be sent and summed in bfloat16 or wider, within the bound.
No kernel may reach another device: no remote copies, remote signals or barrier semaphores. Data moves between devices by JAX's collectives and lax.ppermute only.
A program may use at most 128 MiB of HBM per device.

v0:
```python
import jax
import jax.numpy as jnp
from jax import lax
from jax.sharding import PartitionSpec as P

STEP = 10
beta_one = 0.9
beta_two = 0.999
adam_eps = 1e-08
learn_rate = 0.001
decay_rate = 0.1
scale_eps = 1e-06


def gelu_pair(pre_act):
    cdf_part = 0.5 * (1.0 + lax.erf(pre_act * 0.7071067811865476))
    slope = cdf_part + pre_act * jnp.exp(-0.5 * pre_act * pre_act) * 0.3989422804014327
    return (pre_act * cdf_part, slope)


def spread_scale(values, scale):
    blocks = scale.shape[0]
    shaped = values.reshape(blocks, values.shape[0] // blocks, values.shape[1])
    return (shaped * scale[:, None, :]).reshape(values.shape)


def block_max(values, blocks):
    shaped = values.reshape(blocks, values.shape[0] // blocks, values.shape[1])
    return jnp.max(jnp.abs(shaped), axis=1) + scale_eps


def adam_step(weight, grad_w, mean_q, mean_scale, var_q, var_scale):
    blocks = mean_scale.shape[0]
    mean_new = (
        beta_one * spread_scale(mean_q.astype(jnp.float32), mean_scale) + (1.0 - beta_one) * grad_w
    )
    var_new = (
        beta_two * spread_scale(var_q.astype(jnp.float32), var_scale)
        + (1.0 - beta_two) * grad_w * grad_w
    )
    mean_hat = mean_new / (1.0 - beta_one**STEP)
    var_hat = var_new / (1.0 - beta_two**STEP)
    old_weight = weight.astype(jnp.float32)
    new_weight = (
        old_weight
        - learn_rate * (mean_hat / (jnp.sqrt(var_hat) + adam_eps) + decay_rate * old_weight)
    ).astype(jnp.bfloat16)
    mean_scale_next = block_max(mean_new, blocks)
    var_scale_next = block_max(var_new, blocks)
    mean_next = spread_scale(mean_new, 1.0 / mean_scale_next).astype(jnp.bfloat16)
    var_next = spread_scale(var_new, 1.0 / var_scale_next).astype(jnp.bfloat16)
    return (new_weight, mean_next, mean_scale_next, var_next, var_scale_next)


def contract_first(left, right):
    return lax.dot_general(
        left, right, (((0,), (0,)), ((), ())), preferred_element_type=jnp.float32
    )


def local(
    tokens,
    cotangent,
    w_expand,
    w_reduce,
    expand_mean,
    expand_mean_scale,
    expand_var,
    expand_var_scale,
    reduce_mean,
    reduce_mean_scale,
    reduce_var,
    reduce_var_scale,
):
    token_rows, cot_rows = (
        lax.all_gather(tokens, "col", axis=1, tiled=True),
        lax.all_gather(cotangent, "col", axis=1, tiled=True),
    )
    input_whole, cot_whole = (
        lax.all_to_all(token_rows, "row", split_axis=1, concat_axis=0, tiled=True),
        lax.all_to_all(cot_rows, "row", split_axis=1, concat_axis=0, tiled=True),
    )
    up_panel, down_panel = (
        lax.all_gather(w_expand, "row", axis=0, tiled=True),
        lax.all_gather(w_reduce, "row", axis=0, tiled=True),
    )
    pre_act = jnp.dot(token_rows, up_panel, preferred_element_type=jnp.float32)
    act_grad = jnp.dot(cot_rows, down_panel, preferred_element_type=jnp.float32)
    activated, slope = gelu_pair(pre_act)
    activated = activated.astype(jnp.bfloat16)
    pre_grad = (act_grad * slope).astype(jnp.bfloat16)
    grad_cols = lax.psum_scatter(
        lax.dot_general(
            up_panel, pre_grad, (((1,), (1,)), ((), ())), preferred_element_type=jnp.float32
        ),
        "col",
        scatter_dimension=0,
        tiled=True,
    )
    grad_tokens = grad_cols.T.astype(jnp.bfloat16)
    grad_expand = contract_first(input_whole, lax.all_gather(pre_grad, "row", axis=0, tiled=True))
    grad_reduce = contract_first(cot_whole, lax.all_gather(activated, "row", axis=0, tiled=True))
    first = adam_step(
        w_expand, grad_expand, expand_mean, expand_mean_scale, expand_var, expand_var_scale
    )
    second = adam_step(
        w_reduce, grad_reduce, reduce_mean, reduce_mean_scale, reduce_var, reduce_var_scale
    )
    return (
        grad_tokens,
        first[0],
        first[1],
        first[2],
        first[3],
        first[4],
        second[0],
        second[1],
        second[2],
        second[3],
        second[4],
    )


def solution(mesh):
    placed = (
        P("row", "col"),
        P("row", "col"),
        P("row", "col"),
        P("row", "col"),
        P("row", "col"),
        P("row", "col"),
        P("row", "col"),
        P("row", "col"),
        P("row", "col"),
        P("row", "col"),
        P("row", "col"),
        P("row", "col"),
    )
    return jax.shard_map(
        local,
        mesh=mesh,
        in_specs=placed,
        out_specs=(
            P("row", "col"),
            P("row", "col"),
            P("row", "col"),
            P("row", "col"),
            P("row", "col"),
            P("row", "col"),
            P("row", "col"),
            P("row", "col"),
            P("row", "col"),
            P("row", "col"),
            P("row", "col"),
        ),
        check_vma=False,
    )
```

profile of v0, /device:TPU:8, one launch (start us, length us, event | category | flops | bytes accessed | tf_op | source)
XLA Modules:
  0.0 555.6 jit_solution(1710327823756502407)
XLA Ops:
  10.0 82.9 %all-gather.11.cloned.1.call-done = bf16[256,6144]{0,1:T(8,128)(2,1)} async-done(((bf16[256,192]{0,1:T(8,128)(2,1)}), bf16[256,6144]{0,1:T(8,128)(2,1)}) %all-gather.11.cloned.1.call-update) | async-done | bytes 3145744 | tf_op jit(solution)/shard_map/all_gather | solution.py:76
  92.9 34.3 %all-gather.13.cloned.1.call-done = bf16[6144,384]{1,0:T(8,128)(2,1)} async-done(((bf16[768,384]{1,0:T(8,128)(2,1)}), bf16[6144,384]{1,0:T(8,128)(2,1)}) %all-gather.13.cloned.1.call-update) | async-done | bytes 4718608 | tf_op jit(solution)/shard_map/all_gather | solution.py:84
  127.2 5.8 %multiply_convert_fusion.4 = (bf16[256,384]{1,0:T(8,128)(2,1)}, f32[256,384]{1,0:T(8,128)S(1)}) fusion(bf16[256,6144]{0,1:T(8,128)(2,1)} %all-gather.11.cloned.1.call-done, bf16[6144,384]{1,0:T(8,128)(2,1)} %all-gather.13.cloned.1.call-done), kind=kOutput, calls=%fused_computation.30 | convolution fusion | flops 1208451072 | bytes 8454144 | tf_op jit(solution)/shard_map/dot_general | solution.py:87
  133.1 77.2 %all-gather.7.cloned.1.call-done = bf16[256,6144]{0,1:T(8,128)(2,1)} async-done(((bf16[256,192]{0,1:T(8,128)(2,1)}), bf16[256,6144]{0,1:T(8,128)(2,1)}) %all-gather.7.cloned.1.call-update) | async-done | bytes 3145744 | tf_op jit(solution)/shard_map/all_gather | solution.py:77
  210.2 34.2 %all-gather.9.cloned.1.call-done = bf16[6144,384]{1,0:T(8,128)(2,1)} async-done(((bf16[768,384]{1,0:T(8,128)(2,1)}), bf16[6144,384]{1,0:T(8,128)(2,1)}) %all-gather.9.cloned.1.call-update) | async-done | bytes 4718608 | tf_op jit(solution)/shard_map/all_gather | solution.py:85
  244.4 5.9 %fusion.8 = bf16[256,384]{1,0:T(8,128)(2,1)} fusion(bf16[256,6144]{0,1:T(8,128)(2,1)} %all-gather.7.cloned.1.call-done, bf16[6144,384]{1,0:T(8,128)(2,1)} %all-gather.9.cloned.1.call-done, f32[256,384]{1,0:T(8,128)S(1)} %get-tuple-element.82), kind=kOutput, calls=%fused_computation.24 | convolution fusion | flops 1208942592 | bytes 8454144 | tf_op jit(solution)/shard_map/dot_general | solution.py:88
  250.9 7.0 %convolution_bitcast_fusion = f32[6144,256]{0,1:T(8,128)} fusion(bf16[256,384]{1,0:T(8,128)(2,1)} %fusion.8, bf16[6144,384]{1,0:T(8,128)(2,1)} %all-gather.13.cloned.1.call-done), kind=kOutput, calls=%fused_computation | convolution fusion | flops 1207959552 | bytes 11206656 | tf_op jit(solution)/shard_map/dot_general | solution.py:93
  257.9 6.6 %copy.123 = f32[6144,256]{1,0:T(8,128)} copy(f32[6144,256]{0,1:T(8,128)} %convolution_bitcast_fusion) | data formatting | bytes 12582912
  266.4 49.7 %all_to_all.38 = bf16[256,8,768]{0,2,1:T(8,128)(2,1)} all-to-all(bf16[256,8,768]{0,2,1:T(8,128)(2,1)S(1)} %bitcast.38), channel_id=1, replica_groups=mesh['row'=8,'col'=32] {'row'}, dimensions={1} | all-to-all | bytes 6291456 | tf_op jit(solution)/shard_map/all_to_all | solution.py:80
  316.1 4.0 all-to-all-start.1
  320.2 2.1 copy.96
  325.5 2.7 copy.101
  329.3 2.7 copy.98
  332.0 2.1 copy.100
  337.4 2.7 copy.108
  341.2 2.7 copy.111
  343.8 2.1 copy.107
  346.0 2.1 copy.110
  348.1 4.7 copy.99
  352.8 4.3 all-to-all-done.1
  357.1 2.9 copy.109
  360.0 6.3 %fusion.18 = (f32[768,384]{0,1:T(8,128)}, f32[768,384]{0,1:T(8,128)S(1)}, f32[768,384]{0,1:T(8,128)S(1)}, f32[768,384]{0,1:T(8,128)S(1)}) fusion(f32[768,384]{0,1:T(8,128)} %copy.98, bf16[768,384]{0,1:T(8,128)(2,1)} %copy.97, f32[768,384]{0,1:T(8,128)} %copy.101, bf16[768,384]{0,1:T(8,128)(2,1)} %copy.100, ...), kind=kOutput, calls=%fused_computation.44 | convolution fusion | flops 1211793408 | bytes 12976128 | tf_op jit(solution)/shard_map/dot_general | solution.py:56
  366.3 2.7 copy.102
  377.8 2.7 copy.105
  380.5 3.5 multiply_convert_fusion.2
  384.0 2.3 copy.117
  388.4 2.1 copy.119
  390.5 6.4 %fusion.15 = (f32[768,384]{0,1:T(8,128)}, f32[768,384]{0,1:T(8,128)}, f32[768,384]{0,1:T(8,128)}, f32[768,384]{0,1:T(8,128)}) fusion(f32[768,384]{0,1:T(8,128)} %copy.108, bf16[768,384]{0,1:T(8,128)(2,1)} %copy.107, f32[768,384]{0,1:T(8,128)} %copy.111, bf16[768,384]{0,1:T(8,128)(2,1)} %copy.110, bf16[2048,384]{1,0:T(8,128)(2,1)} %all-gather.17.cloned.1.call-done, ...), kind=kOutput, calls=%fused_computation.42 | convolution fusion | flops 1211793408 | bytes 12976128 | tf_op jit(solution)/shard_map/dot_general | solution.py:56
  402.5 2.9 copy.115
  405.4 3.5 multiply_convert_fusion
  408.9 2.2 copy.120
  413.2 133.7 %reduce-scatter.4.cloned.1.call-done = f32[192,256]{1,0:T(8,128)} async-done(((f32[6144,256]{1,0:T(8,128)}), f32[192,256]{1,0:T(8,128)}) %reduce-scatter.4.cloned.1.call-update) | async-done | bytes 196624
  (66 shorter events, 34.4 us)
Async XLA Ops:
  7.2 85.7 %all-gather.11.cloned.1.call-start = ((), (), s32[]{:S(2)}) async-start(), calls=%async_computation.5 | async-start | bytes 3244032 | tf_op jit(solution)/shard_map/all_gather | solution.py:76
  7.9 119.3 %all-gather.13.cloned.1.call-start = ((), (), s32[]{:S(2)}) async-start(), calls=%async_computation.6 | async-start | bytes 5308416 | tf_op jit(solution)/shard_map/all_gather | solution.py:84
  8.7 201.6 %all-gather.7.cloned.1.call-start = ((), (), s32[]{:S(2)}) async-start(), calls=%async_computation.3 | async-start | bytes 3244032 | tf_op jit(solution)/shard_map/all_gather | solution.py:77
  9.4 235.0 %all-gather.9.cloned.1.call-start = ((), (), s32[]{:S(2)}) async-start(), calls=%async_computation.4 | async-start | bytes 5308416 | tf_op jit(solution)/shard_map/all_gather | solution.py:85
  10.0 350.0 %all-gather.15.cloned.1.call-start = ((), (), s32[]{:S(2)}) async-start(), calls=%async_computation.7 | async-start | bytes 1769472 | tf_op jit(solution)/shard_map/all_gather | solution.py:101
  250.3 140.2 %all-gather.17.cloned.1.call-start = ((), (), s32[]{:S(2)}) async-start(), calls=%async_computation.8 | async-start | bytes 1769472 | tf_op jit(solution)/shard_map/all_gather | solution.py:102
  250.9 296.1 %reduce-scatter.4.cloned.1.call-start = ((), (), s32[]{:S(2)}) async-start(), calls=%async_computation.9 | async-start | bytes 6488064
  264.5 1.9 copy-start
  316.1 41.0 %all-to-all-start.1 = ((bf16[256,8,768]{0,2,1:T(8,128)(2,1)}), bf16[256,8,768]{0,2,1:T(8,128)(2,1)S(1)}, u32[]{:S(2)}, u32[]{:S(2)}) async-start(bf16[256,8,768]{0,2,1:T(8,128)(2,1)} %bitcast.39), calls=%async_computation.1 | async-start | bytes 6291456 | tf_op jit(solution)/shard_map/all_to_all | solution.py:81
  320.2 4.3 copy-start.8
  325.5 2.7 copy-start.9
  332.0 4.3 copy-start.10
  337.4 2.7 copy-start.11
  370.4 1.6 copy-start.5
  384.0 6.5 %copy-start.1 = (bf16[8,256,768]{2,1,0:T(8,128)(2,1)S(1)}, bf16[8,256,768]{2,1,0:T(8,128)(2,1)}, u32[]{:S(2)}) copy-start(bf16[8,256,768]{2,1,0:T(8,128)(2,1)} %copy.109) | copy-start | bytes 9437188
  398.5 1.3 copy-start.4
  402.5 2.9 copy-start.2
  402.5 2.9 copy-start.3
  408.9 2.2 copy-start.7
  408.9 3.3 copy-start.6
Sparse Core Ops, SparseCore 0:
  10.6 82.2 all-gather.10
  94.7 32.4 all-gather.12
  129.8 80.3 all-gather.6
  211.9 32.4 all-gather.8
  250.4 27.9 all-gather.14
  280.1 34.5 all-gather.16
  318.7 228.2 reduce-scatter.3
where the time goes:
time: 557 us; the launch traced here: 556 us
  waiting for transfers between devices  370 us (66%)
  local copies, waits for them, and re-layouts  75.1 us (13%)
  blocking collectives  49.7 us (9%)
  matrix products  31.3 us (6%)
  between operations  14.2 us (3%)
  other arithmetic  11.2 us (2%)
    unnamed x8, waiting for transfers between devices  137 us
    all_gather x1, waiting for transfers between devices, local(): lax.all_gather(tokens, 'col', axis=1, tiled=True)  82.9 us
    all_gather x1, waiting for transfers between devices, local(): lax.all_gather(cotangent, 'col', axis=1, tiled=True)  77.2 us
    all_to_all x1, blocking collectives, local(): lax.all_to_all(token_rows, 'row', split_axis=1, concat_axis=0, tiled=True)  49.7 us
    unnamed x39, local copies, waits for them, and re-layouts  35.3 us
    all_gather x1, waiting for transfers between devices, local(): lax.all_gather(w_expand, 'row', axis=0, tiled=True)  34.3 us
    all_gather x1, waiting for transfers between devices, local(): lax.all_gather(w_reduce, 'row', axis=0, tiled=True)  34.2 us
    mul x16, local copies, waits for them, and re-layouts, spread_scale(): return (shaped * scale[:, None, :]).reshape(values.shape)  26.2 us
  transfers between devices with their start and end apart: 8, of which 6 were waited for; matrix products, arithmetic and copies ran while one was open for 19% of the time, Pallas kernels for 0%

commit v1 on v0

--- a/solution.py
+++ b/solution.py
@@ -10,6 +10,11 @@
 learn_rate = 0.001
 decay_rate = 0.1
 scale_eps = 1e-06
+
+
+def gather_by_exchange(shard, axis, dim):
+    copies = jnp.concatenate([shard] * lax.axis_size(axis), axis=dim)
+    return lax.all_to_all(copies, axis, dim, dim, tiled=True)
 
 
 def gelu_pair(pre_act):
@@ -82,7 +87,7 @@
     )
     up_panel, down_panel = (
         lax.all_gather(w_expand, "row", axis=0, tiled=True),
-        lax.all_gather(w_reduce, "row", axis=0, tiled=True),
+        gather_by_exchange(w_reduce, "row", 0),
     )
     pre_act = jnp.dot(token_rows, up_panel, preferred_element_type=jnp.float32)
     act_grad = jnp.dot(cot_rows, down_panel, preferred_element_type=jnp.float32)

time: 557 us -> 523 us (0.939)
  waiting for transfers between devices: 370 us -> 340 us
  local copies, waits for them, and re-layouts: 75.1 us -> 65 us
  starting transfers between devices: 4.3 us -> 11.4 us
    all_gather x1 -> x0, waiting for transfers between devices: 34.2 us -> none  [local(): lax.all_gather(w_reduce, 'row', axis=0, tiled=True)]
    all_to_all x1, waiting for transfers between devices: 4.32 us -> 17.5 us  [local(): lax.all_to_all(cot_rows, 'row', split_axis=1, concat_axis=0, tiled=True)]
    all_gather x1, waiting for transfers between devices: 82.9 us -> 73.9 us  [local(): lax.all_gather(tokens, 'col', axis=1, tiled=True)]
    all_to_all x0 -> x1, starting transfers between devices: none -> 6.64 us  [gather_by_exchange(): return lax.all_to_all(copies, axis, dim, dim, tiled=True)]
    mul x16, local copies, waits for them, and re-layouts: 26.2 us -> 20.5 us  [spread_scale(): return (shaped * scale[:, None, :]).reshape(values.shape)]
    unnamed x39 -> x54, local copies, waits for them, and re-layouts: 35.3 us -> 30.7 us
    unnamed x8 -> x7, waiting for transfers between devices: 137 us -> 137 us
  transfers between devices with their start and end apart: 8 -> 8, of which waited for: 6 -> 5; matrix products, arithmetic and copies ran while one was open for 19% -> 19% of each run, Pallas kernels for 0% -> 0%
where the time goes in v1:
time: 523 us; the launch traced here: 522 us
  waiting for transfers between devices  340 us (65%)
  local copies, waits for them, and re-layouts  65 us (12%)
  blocking collectives  47.2 us (9%)
  matrix products  31.9 us (6%)
  between operations  14.4 us (3%)
  other arithmetic  12.2 us (2%)
  starting transfers between devices  11.4 us (2%)
    unnamed x7, waiting for transfers between devices  137 us
    all_gather x1, waiting for transfers between devices, local(): lax.all_gather(cotangent, 'col', axis=1, tiled=True)  77.1 us
    all_gather x1, waiting for transfers between devices, local(): lax.all_gather(tokens, 'col', axis=1, tiled=True)  73.9 us
    all_to_all x1, blocking collectives, local(): lax.all_to_all(token_rows, 'row', split_axis=1, concat_axis=0, tiled=True)  47.2 us
    all_gather x1, waiting for transfers between devices, local(): lax.all_gather(w_expand, 'row', axis=0, tiled=True)  34.3 us
    unnamed x54, local copies, waits for them, and re-layouts  30.7 us
    mul x16, local copies, waits for them, and re-layouts, spread_scale(): return (shaped * scale[:, None, :]).reshape(values.shape)  20.5 us
    all_to_all x1, waiting for transfers between devices, local(): lax.all_to_all(cot_rows, 'row', split_axis=1, concat_axis=0, tiled=True)  17.5 us
  transfers between devices with their start and end apart: 8, of which 5 were waited for; matrix products, arithmetic and copies ran while one was open for 19% of the time, Pallas kernels for 0%

profile of v1, /device:TPU:8, one launch (start us, length us, event | category | flops | bytes accessed | tf_op | source)
XLA Modules:
  0.0 521.7 jit_solution(8183200439814048404)
XLA Ops:
  10.2 2.2 copy-done.5
  12.4 6.6 %all-to-all-start = ((bf16[8,768,384]{2,1,0:T(8,128)(2,1)}), bf16[8,768,384]{2,1,0:T(8,128)(2,1)}, u32[]{:S(2)}, u32[]{:S(2)}) async-start(bf16[8,768,384]{2,1,0:T(8,128)(2,1)} %bitcast.50), calls=%async_computation | async-start | bytes 9437184 | tf_op jit(solution)/shard_map/all_to_all | solution.py:17
  19.0 73.9 %all-gather.8.cloned.1.call-done = bf16[256,6144]{0,1:T(8,128)(2,1)} async-done(((bf16[256,192]{0,1:T(8,128)(2,1)}), bf16[256,6144]{0,1:T(8,128)(2,1)}) %all-gather.8.cloned.1.call-update) | async-done | bytes 3145744 | tf_op jit(solution)/shard_map/all_gather | solution.py:81
  92.9 34.3 %all-gather.10.cloned.1.call-done = bf16[6144,384]{1,0:T(8,128)(2,1)} async-done(((bf16[768,384]{1,0:T(8,128)(2,1)}), bf16[6144,384]{1,0:T(8,128)(2,1)}) %all-gather.10.cloned.1.call-update) | async-done | bytes 4718608 | tf_op jit(solution)/shard_map/all_gather | solution.py:89
  127.2 5.9 %multiply_convert_fusion.4 = (bf16[256,384]{0,1:T(8,128)(2,1)}, f32[256,384]{0,1:T(8,128)S(1)}) fusion(bf16[256,6144]{0,1:T(8,128)(2,1)} %all-gather.8.cloned.1.call-done, bf16[6144,384]{1,0:T(8,128)(2,1)} %all-gather.10.cloned.1.call-done), kind=kOutput, calls=%fused_computation.31 | convolution fusion | flops 1208451072 | bytes 8454144 | tf_op jit(solution)/shard_map/dot_general | solution.py:92
  133.2 77.1 %all-gather.6.cloned.1.call-done = bf16[256,6144]{0,1:T(8,128)(2,1)} async-done(((bf16[256,192]{0,1:T(8,128)(2,1)}), bf16[256,6144]{0,1:T(8,128)(2,1)}) %all-gather.6.cloned.1.call-update) | async-done | bytes 3145744 | tf_op jit(solution)/shard_map/all_gather | solution.py:82
  210.3 5.4 %fusion.9 = bf16[256,384]{0,1:T(8,128)(2,1)} fusion(bf16[6144,384]{1,0:T(8,128)(2,1)} %bitcast.1, bf16[256,6144]{0,1:T(8,128)(2,1)} %all-gather.6.cloned.1.call-done, f32[256,384]{0,1:T(8,128)S(1)} %get-tuple-element.82), kind=kOutput, calls=%fused_computation.25 | convolution fusion | flops 1208942592 | bytes 8454144 | tf_op jit(solution)/shard_map/dot_general | solution.py:93
  216.4 7.0 %convolution_bitcast_fusion = f32[6144,256]{0,1:T(8,128)} fusion(bf16[256,384]{0,1:T(8,128)(2,1)} %fusion.9, bf16[6144,384]{1,0:T(8,128)(2,1)} %all-gather.10.cloned.1.call-done), kind=kOutput, calls=%fused_computation | convolution fusion | flops 1207959552 | bytes 11206656 | tf_op jit(solution)/shard_map/dot_general | solution.py:98
  223.3 6.7 %copy.144 = f32[6144,256]{1,0:T(8,128)} copy(f32[6144,256]{0,1:T(8,128)} %convolution_bitcast_fusion) | data formatting | bytes 12582912
  230.0 47.2 %all_to_all.50 = bf16[256,8,768]{0,2,1:T(8,128)(2,1)} all-to-all(bf16[256,8,768]{0,2,1:T(8,128)(2,1)} %bitcast.63), channel_id=1, replica_groups=mesh['row'=8,'col'=32] {'row'}, dimensions={1} | all-to-all | bytes 6291456 | tf_op jit(solution)/shard_map/all_to_all | solution.py:85
  277.2 4.5 all-to-all-start.2
  286.6 1.4 copy.120
  292.7 2.8 copy.131
  295.5 2.1 copy.130
  297.7 2.9 copy.118
  300.5 17.5 %all-to-all-done.2 = bf16[256,8,768]{0,2,1:T(8,128)(2,1)} async-done(((bf16[256,8,768]{0,2,1:T(8,128)(2,1)}), bf16[256,8,768]{0,2,1:T(8,128)(2,1)}, u32[]{:S(2)}, u32[]{:S(2)}) %all-to-all-start.2) | async-done | bytes 3145760 | tf_op jit(solution)/shard_map/all_to_all | solution.py:86
  318.0 3.4 copy.129
  321.4 7.3 %fusion.19 = (f32[768,384]{0,1:T(8,128)}, f32[768,384]{0,1:T(8,128)}, f32[768,384]{0,1:T(8,128)}, f32[768,384]{0,1:T(8,128)}) fusion(f32[768,384]{0,1:T(8,128)} %copy.117, bf16[768,384]{0,1:T(8,128)(2,1)} %copy.116, f32[768,384]{0,1:T(8,128)} %copy.120, bf16[768,384]{0,1:T(8,128)(2,1)} %copy.119, bf16[2048,384]{0,1:T(8,128)(2,1)} %all-gather.12.cloned.1.call-done, ...), kind=kOutput, calls=%fused_computation.53 | convolution fusion | flops 1211793408 | bytes 12976128 | tf_op jit(solution)/shard_map/dot_general | solution.py:61
  328.7 2.7 copy.123
  331.4 2.7 copy.121
  338.5 2.7 copy.124
  342.4 2.7 copy.122
  345.1 4.6 multiply_convert_fusion.2
  349.7 2.1 copy.137
  351.8 2.1 copy.138
  353.9 2.1 copy.139
  356.1 6.3 %fusion.16 = (f32[768,384]{0,1:T(8,128)}, f32[768,384]{0,1:T(8,128)}, f32[768,384]{0,1:T(8,128)}, f32[768,384]{0,1:T(8,128)}) fusion(f32[768,384]{0,1:T(8,128)} %copy.127, bf16[768,384]{0,1:T(8,128)(2,1)} %copy.126, f32[768,384]{0,1:T(8,128)} %copy.131, bf16[768,384]{0,1:T(8,128)(2,1)} %copy.130, bf16[2048,384]{0,1:T(8,128)(2,1)} %all-gather.14.cloned.1.call-done, ...), kind=kOutput, calls=%fused_computation.51 | convolution fusion | flops 1211793408 | bytes 12976128 | tf_op jit(solution)/shard_map/dot_general | solution.py:61
  362.4 1.6 copy.134
  368.0 2.9 copy.133
  370.9 3.5 multiply_convert_fusion
  374.4 2.2 copy.140
  378.8 134.3 %reduce-scatter.4.cloned.1.call-done = f32[192,256]{1,0:T(8,128)} async-done(((f32[6144,256]{1,0:T(8,128)}), f32[192,256]{1,0:T(8,128)}) %reduce-scatter.4.cloned.1.call-update) | async-done | bytes 196624
  (81 shorter events, 26.5 us)
Async XLA Ops:
  7.2 2.2 copy-start
  7.2 85.7 %all-gather.8.cloned.1.call-start = ((), (), s32[]{:S(2)}) async-start(), calls=%async_computation.5 | async-start | bytes 3244032 | tf_op jit(solution)/shard_map/all_gather | solution.py:81
  7.9 119.3 %all-gather.10.cloned.1.call-start = ((), (), s32[]{:S(2)}) async-start(), calls=%async_computation.6 | async-start | bytes 5308416 | tf_op jit(solution)/shard_map/all_gather | solution.py:89
  8.7 201.6 %all-gather.6.cloned.1.call-start = ((), (), s32[]{:S(2)}) async-start(), calls=%async_computation.4 | async-start | bytes 3244032 | tf_op jit(solution)/shard_map/all_gather | solution.py:82
  10.2 2.2 copy-start.5
  12.4 120.8 %all-to-all-start = ((bf16[8,768,384]{2,1,0:T(8,128)(2,1)}), bf16[8,768,384]{2,1,0:T(8,128)(2,1)}, u32[]{:S(2)}, u32[]{:S(2)}) async-start(bf16[8,768,384]{2,1,0:T(8,128)(2,1)} %bitcast.50), calls=%async_computation | async-start | bytes 9437184 | tf_op jit(solution)/shard_map/all_to_all | solution.py:17
  19.0 302.4 %all-gather.12.cloned.1.call-start = ((), (), s32[]{:S(2)}) async-start(), calls=%async_computation.7 | async-start | bytes 1769472 | tf_op jit(solution)/shard_map/all_gather | solution.py:106
  215.7 140.4 %all-gather.14.cloned.1.call-start = ((), (), s32[]{:S(2)}) async-start(), calls=%async_computation.8 | async-start | bytes 1769472 | tf_op jit(solution)/shard_map/all_gather | solution.py:107
  216.3 296.7 %reduce-scatter.4.cloned.1.call-start = ((), (), s32[]{:S(2)}) async-start(), calls=%async_computation.9 | async-start | bytes 6488064
  277.2 4.5 copy-start.8
  277.2 40.8 %all-to-all-start.2 = ((bf16[256,8,768]{0,2,1:T(8,128)(2,1)}), bf16[256,8,768]{0,2,1:T(8,128)(2,1)}, u32[]{:S(2)}, u32[]{:S(2)}) async-start(bf16[256,8,768]{0,2,1:T(8,128)(2,1)} %bitcast.46), calls=%async_computation.2 | async-start | bytes 6291456 | tf_op jit(solution)/shard_map/all_to_all | solution.py:86
  281.7 2.2 copy-start.12
  284.0 1.4 copy-start.9
  285.4 1.1 copy-start.13
  286.6 1.5 copy-start.10
  288.0 1.1 copy-start.14
  289.2 1.4 copy-start.11
  290.6 1.1 copy-start.15
  292.7 5.0 copy-start.1
  364.0 1.3 copy-start.4
  368.0 2.9 copy-start.2
  368.0 2.9 copy-start.3
  374.4 2.2 copy-start.7
  374.4 3.3 copy-start.6
Sparse Core Ops, SparseCore 0:
  10.6 82.2 all-gather.7
  94.7 32.4 all-gather.9
  129.8 80.3 all-gather.5
  215.8 25.6 all-gather.11
  243.2 39.1 all-gather.13
  286.2 226.7 reduce-scatter.3
